TPU v7x, 128 devices: a whole 4x4x4 slice. The times are simulated.
128 devices in a mesh: dp: 8 (over y, core), mp: 16 (over x, z).
Axes of the slice: x: 4, y: 4, z: 4, core: 2. Of those that a mesh axis runs over, the one named last changes fastest.
Arguments:
- span_tokens: bfloat16 [128, 256, 2560], P(('dp', 'mp')), may hold values from -6 to 6
- decode_tokens: bfloat16 [256, 2560], P(('dp', 'mp')), may hold values from -6 to 6
- norm_gain: float32 [2560], replicated, may hold values from 0.5 to 1.5
- query_weight: bfloat16 [2560, 2560], P(('dp', 'mp')), may hold values from -0.125 to 0.125
- keyval_weight: bfloat16 [2560, 512], P(('dp', 'mp')), may hold values from -0.125 to 0.125
- output_weight: bfloat16 [2560, 2560], P(('dp', 'mp')), may hold values from -0.125 to 0.125
- span_cache: bfloat16 [128, 2048, 512], P(('dp', 'mp')), may hold values from -360 to 360
- decode_cache: bfloat16 [256, 2048, 512], P(('dp', 'mp')), may hold values from -360 to 360
- span_index: int32 [128], P(('dp', 'mp')), may hold values from 0 to 15
- decode_length: int32 [256], P(('dp', 'mp')), may hold values from 1 to 32768
- cache_slot: int32 [256], replicated, may hold values from 0 to 255, each once
Outputs:
- span_output: bfloat16 [128, 256, 2560], P(('dp', 'mp'))
- span_keyval: bfloat16 [128, 256, 512], P(('dp', 'mp'))
- decode_output: bfloat16 [256, 2560], P(('dp', 'mp'))
- decode_keyval: bfloat16 [256, 512], P(('dp', 'mp'))
Inputs may be any that keep to these rules, and one draw needn't show every extreme that they name: `cache_slot`: each cache slot belongs to exactly one request.
All inputs are finite; a program needn't handle non-finite values.
Results may differ from a plain program's by a relative error of at most 0.024.
Values may be sent and summed in bfloat16 or wider, within the bound.
No kernel may reach another device: no remote copies, remote signals or barrier semaphores. Data moves between devices by JAX's collectives and lax.ppermute only.
A program may use at most 128 MiB of HBM per device.

v0:
```python
import jax
import jax.numpy as jnp
from jax import lax
from jax.sharding import PartitionSpec as P


def rms_normed(rows_in, norm_gain):
    widened = rows_in.astype(jnp.float32)
    spread = jnp.mean(widened * widened, axis=-1, keepdims=True)
    return (widened * lax.rsqrt(spread + 1e-06) * norm_gain).astype(jnp.bfloat16)


def rotate(values, positions):
    quarter = values.shape[-1] // 4
    frequency = 10000.0 ** (-jnp.arange(quarter, dtype=jnp.float32) / quarter)
    angles = positions.astype(jnp.float32)[..., None] * frequency
    cos_part = jnp.cos(angles)
    sin_part = jnp.sin(angles)
    first_half = values[..., :quarter]
    second_half = values[..., quarter : 2 * quarter]
    return jnp.concatenate(
        [
            first_half * cos_part - second_half * sin_part,
            second_half * cos_part + first_half * sin_part,
            values[..., 2 * quarter :],
        ],
        -1,
    )


def span_attend(queries, keyval, stored, offset):
    head_dim = queries.shape[-1]
    length = queries.shape[0]
    window = stored.shape[0]
    key_rows = jnp.concatenate([stored[:, :head_dim], keyval[:, :head_dim]], 0)
    value_rows = jnp.concatenate([stored[:, head_dim:], keyval[:, head_dim:]], 0)
    row_ids = jnp.arange(length, dtype=jnp.int32)
    slot_ids = jnp.arange(window, dtype=jnp.int32)
    held_pos = offset - 1 - jnp.mod(offset - 1 - slot_ids, window)
    cache_ok = (held_pos[None, :] >= 0) & (
        held_pos[None, :] >= offset + row_ids[:, None] - window + 1
    )
    own_ok = row_ids[None, :] <= row_ids[:, None]
    allowed = jnp.concatenate([cache_ok, own_ok], 1)

    def one_head(head_queries):
        scores = jnp.dot(
            head_queries, key_rows.T, preferred_element_type=jnp.float32
        ) * head_dim ** (-0.5)
        highest = jnp.max(jnp.where(allowed, scores, -1e30), -1, keepdims=True)
        exp_terms = jnp.where(allowed, jnp.exp(scores - highest), 0.0)
        weights = (exp_terms / jnp.sum(exp_terms, -1, keepdims=True)).astype(jnp.bfloat16)
        return jnp.dot(weights, value_rows, preferred_element_type=jnp.float32).astype(jnp.bfloat16)

    per_head = lax.map(one_head, jnp.transpose(queries, (1, 0, 2)))
    return jnp.transpose(per_head, (1, 0, 2)).reshape(length, -1)


def decode_attend(queries, keyval, stored, length):
    head_dim = queries.shape[-1]
    window = stored.shape[1]
    score_scale = head_dim ** (-0.5)
    exp_scores = (
        jnp.einsum(
            "ehd,ewd->ehw", queries, stored[..., :head_dim], preferred_element_type=jnp.float32
        )
        * score_scale
    )
    self_scores = (
        jnp.einsum("ehd,ed->eh", queries, keyval[:, :head_dim], preferred_element_type=jnp.float32)
        * score_scale
    )
    slot_ids = jnp.arange(window, dtype=jnp.int32)
    allowed = (slot_ids[None, :] < length[:, None]) & (
        slot_ids[None, :] != jnp.mod(length, window)[:, None]
    )
    allowed = allowed[:, None, :]
    highest = jnp.maximum(jnp.max(jnp.where(allowed, exp_scores, -1e30), -1), self_scores)
    exp_cache = jnp.where(allowed, jnp.exp(exp_scores - highest[..., None]), 0.0)
    exp_self = jnp.exp(self_scores - highest)
    denominator = jnp.sum(exp_cache, -1) + exp_self
    weight_cache = (exp_cache / denominator[..., None]).astype(jnp.bfloat16)
    weight_self = (exp_self / denominator).astype(jnp.bfloat16)
    attended = jnp.einsum(
        "ehw,ewd->ehd", weight_cache, stored[..., head_dim:], preferred_element_type=jnp.float32
    )
    attended = attended + weight_self.astype(jnp.float32)[..., None] * keyval[
        :, None, head_dim:
    ].astype(jnp.float32)
    return attended.astype(jnp.bfloat16).reshape(queries.shape[0], -1)


def shards(
    span_tokens,
    decode_tokens,
    norm_gain,
    query_weight,
    keyval_weight,
    output_weight,
    span_cache,
    decode_cache,
    span_index,
    decode_length,
    cache_slot,
):
    span_len = span_tokens.shape[1]
    own_slots = decode_cache.shape[0]
    requests = cache_slot.shape[0]
    head_dim = keyval_weight.shape[1] // 2
    device = lax.axis_index(("dp", "mp"))
    arrived, arrived_len = (
        lax.all_gather(decode_tokens, ("dp", "mp"), axis=0, tiled=True),
        lax.all_gather(decode_length, ("dp", "mp"), axis=0, tiled=True),
    )
    slot_ids = device * own_slots + jnp.arange(own_slots, dtype=jnp.int32)
    picker = cache_slot[None, :] == slot_ids[:, None]
    own_tokens = jnp.dot(
        picker.astype(jnp.bfloat16), arrived, preferred_element_type=jnp.float32
    ).astype(jnp.bfloat16)
    own_length = jnp.sum(jnp.where(picker, arrived_len[None, :], 0), axis=1).astype(jnp.int32)
    offset = span_index[0] * span_len
    positions = jnp.concatenate([offset + jnp.arange(span_len, dtype=jnp.int32), own_length])
    rows_all = jnp.concatenate([span_tokens[0], own_tokens], 0)
    normed = rms_normed(rows_all, norm_gain)
    row_count = rows_all.shape[0]
    columns = normed
    query_all = jnp.dot(
        columns,
        lax.all_gather(query_weight, ("dp", "mp"), axis=0, tiled=True),
        preferred_element_type=jnp.float32,
    )
    keyval_all = jnp.dot(
        columns,
        lax.all_gather(keyval_weight, ("dp", "mp"), axis=0, tiled=True),
        preferred_element_type=jnp.float32,
    )
    queries = rotate(query_all.reshape(row_count, -1, head_dim), positions[:, None]).astype(
        jnp.bfloat16
    )
    key_rows = rotate(keyval_all[:, :head_dim], positions).astype(jnp.bfloat16)
    keyval = jnp.concatenate([key_rows, keyval_all[:, head_dim:].astype(jnp.bfloat16)], 1)
    span_mixed = span_attend(queries[:span_len], keyval[:span_len], span_cache[0], offset)
    decode_mixed = decode_attend(queries[span_len:], keyval[span_len:], decode_cache, own_length)
    attended = jnp.concatenate([span_mixed, decode_mixed], 0)
    columns = attended
    projected = jnp.dot(
        columns,
        lax.all_gather(output_weight, ("dp", "mp"), axis=0, tiled=True),
        preferred_element_type=jnp.float32,
    )
    finished = (rows_all.astype(jnp.float32) + projected).astype(jnp.bfloat16)
    span_output = finished[:span_len][None]
    span_keyval = keyval[:span_len][None]
    served = finished[span_len:]
    decode_keyval = keyval[span_len:]
    everything = lax.all_gather(served, ("dp", "mp"), axis=0, tiled=True)
    arriving_slots = lax.dynamic_slice_in_dim(cache_slot, device * own_slots, own_slots)
    chooser = arriving_slots[:, None] == jnp.arange(requests, dtype=jnp.int32)[None, :]
    decode_output = jnp.dot(
        chooser.astype(jnp.bfloat16), everything, preferred_element_type=jnp.float32
    ).astype(jnp.bfloat16)
    return (span_output, span_keyval, decode_output, decode_keyval)


def solution(mesh):
    return jax.shard_map(
        shards,
        mesh=mesh,
        in_specs=(
            P(("dp", "mp"), None, None),
            P(("dp", "mp"), None),
            P(),
            P(("dp", "mp"), None),
            P(("dp", "mp"), None),
            P(("dp", "mp"), None),
            P(("dp", "mp"), None, None),
            P(("dp", "mp"), None, None),
            P(("dp", "mp")),
            P(("dp", "mp")),
            P(),
        ),
        out_specs=(
            P(("dp", "mp"), None, None),
            P(("dp", "mp"), None, None),
            P(("dp", "mp"), None),
            P(("dp", "mp"), None),
        ),
        check_vma=False,
    )
```

profile of v0, /device:TPU:1, one launch (start us, length us, event | category | flops | bytes accessed | tf_op | source)
XLA Modules:
  0.0 406.3 jit_solution(6080341818031185715)
XLA Ops:
  11.5 69.1 %all-reduce = s32[256]{0:T(256)S(1)} all-reduce(s32[256]{0:T(256)S(1)} %dynamic-update-slice), channel_id=1, replica_groups=mesh['dp'=8,'mp'=16] {'dp','mp'}, use_global_device_ids=true, to_apply=%add | all-reduce | flops 256 | bytes 2048
  82.2 2.7 fusion.54
  84.8 3.2 reshape.227
  89.7 55.2 %all-gather.15.cloned.1.call-done = bf16[128,20,512]{2,1,0:T(8,128)(2,1)} async-done(((bf16[1,20,512]{2,1,0:T(8,128)(2,1)}), bf16[128,20,512]{2,1,0:T(8,128)(2,1)}) %all-gather.15.cloned.1.call-update) | async-done | bytes 2621456 | tf_op jit(solution)/shard_map/all_gather | solution.py:134
  144.9 5.2 %reshape.231 = bf16[2560,512]{1,0:T(8,128)(2,1)} reshape(bf16[128,20,512]{2,1,0:T(8,128)(2,1)} %all-gather.15.cloned.1.call-done) | data formatting | bytes 5242880
  150.1 2.7 fusion.55
  152.9 1.3 subtract_convert_fusion.1
  154.4 1.2 pad_maximum_fusion.2
  155.6 68.3 %all-gather.13.cloned.1.call-done = bf16[128,20,2560]{2,1,0:T(8,128)(2,1)} async-done(((bf16[1,20,2560]{2,1,0:T(8,128)(2,1)}), bf16[128,20,2560]{2,1,0:T(8,128)(2,1)}) %all-gather.13.cloned.1.call-update) | async-done | bytes 13107216 | tf_op jit(solution)/shard_map/all_gather | solution.py:129
  223.8 18.0 %reshape.229 = bf16[2560,2560]{1,0:T(8,128)(2,1)} reshape(bf16[128,20,2560]{2,1,0:T(8,128)(2,1)} %all-gather.13.cloned.1.call-done) | data formatting | bytes 26214400
  241.8 8.5 %fusion.52 = f32[258,2560]{1,0:T(8,128)} fusion(bf16[2560,2560]{1,0:T(8,128)(2,1)} %reshape.229, f32[2560]{0:T(1024)S(1)} %copy-done.12, f32[258]{0:T(512)S(1)} %add_rsqrt_fusion, bf16[2,2560]{1,0:T(2,128)(2,1)S(1)} %convolution_convert_fusion.1, bf16[256,2560]{1,0:T(8,128)(2,1)S(1)} %bitcast.48), kind=kOutput, calls=%fused_computation.102 | convolution fusion | flops 3386280960 | bytes 17081352 | tf_op jit(solution)/shard_map/dot_general | solution.py:127
  250.3 4.5 %reshape.221 = f32[258,10,256]{2,1,0:T(8,128)} reshape(f32[258,2560]{1,0:T(8,128)} %fusion.52) | data formatting | bytes 5283840 | tf_op jit(solution)/shard_map/reshape | solution.py:137
  254.8 1.8 slice.140
  256.6 3.1 subtract_convert_fusion
  259.7 1.1 maximum_bitcast_fusion
  261.4 1.7 copy-done.6
  264.5 1.2 copy.27
  265.7 35.7 %while.10 = (s32[]{:T(128)}, bf16[10,256,256]{1,2,0:T(8,128)(2,1)}, bf16[10,256,256]{2,1,0:T(8,128)(2,1)S(1)}, bf16[2304,256]{1,0:T(8,128)(2,1)S(1)}, pred[256,2...) while((s32[]{:T(128)}, bf16[10,256,256]{1,2,0:T(8,128)(2,1)}, ...), condition=%wide.region_5.6_spmd, body=%wide.region_2.5_spmd.sunk | while | flops 609943040 | bytes 16717421 | solution.py:55
  301.4 3.2 all-gather.17.cloned.1.call-done
  304.7 18.0 %reshape.233 = bf16[2560,2560]{1,0:T(8,128)(2,1)} reshape(bf16[128,20,2560]{2,1,0:T(8,128)(2,1)} %all-gather.17.cloned.1.call-done) | data formatting | bytes 26214400
  322.6 8.8 %fusion.8 = bf16[258,2560]{1,0:T(8,128)(2,1)S(1)} fusion(bf16[2560,2560]{1,0:T(8,128)(2,1)} %reshape.233, bf16[2,2560]{0,1:T(8,128)(2,1)S(1)} %bitcast.50, bf16[256,2560]{0,1:T(8,128)(2,1)} %bitcast.57, bf16[2,2560]{1,0:T(2,128)(2,1)S(1)} %convolution_convert_fusion.1, bf16[256,2560]{1,0:T(8,128)(2,1)S(1)} %bitcast.49), kind=kOutput, calls=%fused_computation.16 | convolution fusion | flops 3388262400 | bytes 17070080 | tf_op jit(solution)/shard_map/dot_general | solution.py:146
  334.7 1.1 slice_bitcast_fusion
  335.8 59.9 %all-gather.19.cloned.1.call-done = bf16[128,2,2560]{2,1,0:T(2,128)(2,1)} async-done(((bf16[1,2,2560]{2,1,0:T(2,128)(2,1)}), bf16[128,2,2560]{2,1,0:T(2,128)(2,1)}) %all-gather.19.cloned.1.call-update) | async-done | bytes 1310736 | tf_op jit(solution)/shard_map/all_gather | solution.py:156
  395.7 3.2 reshape.235
  (143 shorter events, 48.7 us)
Async XLA Ops:
  7.2 77.7 %all-gather.11.cloned.1.call-start = ((), (), s32[]{:S(2)}) async-start(), calls=%async_computation | async-start | bytes 1320960 | tf_op jit(solution)/shard_map/all_gather | solution.py:112
  7.9 137.0 %all-gather.15.cloned.1.call-start = ((), (), s32[]{:S(2)}) async-start(), calls=%async_computation.2 | async-start | bytes 3170304 | tf_op jit(solution)/shard_map/all_gather | solution.py:134
  8.6 215.2 %all-gather.13.cloned.1.call-start = ((), (), s32[]{:S(2)}) async-start(), calls=%async_computation.1 | async-start | bytes 15851520 | tf_op jit(solution)/shard_map/all_gather | solution.py:129
  9.4 295.3 %all-gather.17.cloned.1.call-start = ((), (), s32[]{:S(2)}) async-start(), calls=%async_computation.3 | async-start | bytes 15851520 | tf_op jit(solution)/shard_map/all_gather | solution.py:148
  10.0 385.7 %all-gather.19.cloned.1.call-start = ((), (), s32[]{:S(2)}) async-start(), calls=%async_computation.4 | async-start | bytes 1320960 | tf_op jit(solution)/shard_map/all_gather | solution.py:156
  84.8 3.2 copy-start.11
  88.0 1.3 copy-start.1
  89.7 60.4 %copy-start.2 = (bf16[1,256,2560]{2,1,0:T(8,128)(2,1)S(1)}, bf16[1,256,2560]{2,1,0:T(8,128)(2,1)}, u32[]{:S(2)}) copy-start(bf16[1,256,2560]{2,1,0:T(8,128)(2,1)} %param.13) | copy-start | bytes 3932164
  89.7 60.4 %copy-start.12 = (f32[2560]{0:T(1024)S(1)}, f32[2560]{0:T(1024)}, u32[]{:S(2)}) copy-start(f32[2560]{0:T(1024)} %param.15) | copy-start | bytes 30724
  152.8 1.6 copy-start.8
  152.8 1.6 copy-start
  155.6 86.3 %copy-start.3 = (bf16[1,256,2560]{2,1,0:T(8,128)(2,1)S(1)}, bf16[1,256,2560]{2,1,0:T(8,128)(2,1)}, u32[]{:S(2)}) copy-start(bf16[1,256,2560]{2,1,0:T(8,128)(2,1)} %param.13) | copy-start | bytes 3932164
  254.8 1.8 copy-start.9
  254.8 1.8 copy-start.10
  260.8 2.3 copy-start.6
  266.4 1.3 copy-start.5
  273.5 1.3 copy-start.5
  277.0 1.6 copy-start.5
  280.9 1.3 copy-start.5
  284.4 1.3 copy-start.5
  287.9 1.3 copy-start.5
  291.5 1.3 copy-start.5
  301.4 21.2 %copy-start.4 = (bf16[1,256,2560]{2,1,0:T(8,128)(2,1)S(1)}, bf16[1,256,2560]{2,1,0:T(8,128)(2,1)}, u32[]{:S(2)}) copy-start(bf16[1,256,2560]{2,1,0:T(8,128)(2,1)} %param.13) | copy-start | bytes 3932164
  301.4 21.2 %copy-start.7 = (bf16[2,10,256]{0,2,1:T(8,128)(2,1)S(1)}, bf16[2,10,256]{0,2,1:T(8,128)(2,1)}, u32[]{:S(2)}) copy-start(bf16[2,10,256]{0,2,1:T(8,128)(2,1)} %copy.27) | copy-start | bytes 30724
  (3 other events, 3.8 us)
Sparse Core Ops, SparseCore 0:
  10.8 67.5 all-gather.10
  81.5 63.4 all-gather.14
  148.0 75.7 all-gather.12
  226.8 77.8 all-gather.16
  332.2 63.3 all-gather.18
where the time goes:
time: 408 us; the launch traced here: 406 us
  waiting for transfers between devices  189 us (46%)
  local copies, waits for them, and re-layouts  78.9 us (19%)
  blocking collectives  69.1 us (17%)
  matrix products  37.4 us (9%)
  other arithmetic  16.6 us (4%)
  between operations  14.7 us (4%)
    unnamed x1, blocking collectives  69.1 us
    all_gather x1, waiting for transfers between devices, shards(): lax.all_gather(query_weight, ('dp', 'mp'), axis=0, tiled=True)  68.3 us
    all_gather x1, waiting for transfers between devices, shards(): everything = lax.all_gather(served, ('dp', 'mp'), axis=0, tiled=True)  59.9 us
    all_gather x1, waiting for transfers between devices, shards(): lax.all_gather(keyval_weight, ('dp', 'mp'), axis=0, tiled=True)  55.2 us
    unnamed x32, local copies, waits for them, and re-layouts  51.7 us
    dot_general x1, matrix products, shards(): jnp.dot(columns, lax.all_gather(output_weight, ('dp', 'mp'), axis=0, tile...  8.85 us
    dot_general x1, matrix products, shards(): jnp.dot(columns, lax.all_gather(query_weight, ('dp', 'mp'), axis=0, tiled...  8.51 us
  transfers between devices with their start and end apart: 5, of which 4 were waited for; matrix products, arithmetic and copies ran while one was open for 23% of the time, Pallas kernels for 0%

commit v1 on v0

--- a/solution.py
+++ b/solution.py
@@ -1,7 +1,18 @@
+import functools
 import jax
 import jax.numpy as jnp
 from jax import lax
 from jax.sharding import PartitionSpec as P
+
+
+def track_the_scales(s0, a_name, on_dim):
+    finding = lax.psum(1, axis_name=a_name)
+    base_arr = jnp.stack(finding * [s0], axis=0)
+    k_now = lax.all_to_all(base_arr, axis_name=a_name, split_axis=0, concat_axis=0)
+    return jnp.concatenate(k_now, axis=on_dim)
+
+
+link_matrix = functools.partial(track_the_scales, a_name=("dp", "mp"), on_dim=0)
 
 
 def rms_normed(rows_in, norm_gain):
@@ -129,11 +140,7 @@
         lax.all_gather(query_weight, ("dp", "mp"), axis=0, tiled=True),
         preferred_element_type=jnp.float32,
     )
-    keyval_all = jnp.dot(
-        columns,
-        lax.all_gather(keyval_weight, ("dp", "mp"), axis=0, tiled=True),
-        preferred_element_type=jnp.float32,
-    )
+    keyval_all = jnp.dot(columns, link_matrix(keyval_weight), preferred_element_type=jnp.float32)
     queries = rotate(query_all.reshape(row_count, -1, head_dim), positions[:, None]).astype(
         jnp.bfloat16
     )

time: 408 us -> 364 us (0.89)
  waiting for transfers between devices: 189 us -> 108 us
  blocking collectives: 69.1 us -> 92.5 us
  starting transfers between devices: 0.19 us -> 12.1 us
    all_gather x1 -> x0, waiting for transfers between devices: 55.2 us -> none  [shards(): lax.all_gather(keyval_weight, ('dp', 'mp'), axis=0, tiled=True)]
    all_gather x1, waiting for transfers between devices: 68.3 us -> 42.3 us  [shards(): lax.all_gather(query_weight, ('dp', 'mp'), axis=0, tiled=True)]
    unnamed x1, blocking collectives: 69.1 us -> 92.5 us
    all_to_all x0 -> x1, starting transfers between devices: none -> 11.9 us  [track_the_scales(): lax.all_to_all(base_arr, axis_name=a_name, split_axis=0, concat_axis=0)]
    unnamed x32 -> x33, local copies, waits for them, and re-layouts: 51.7 us -> 45.8 us
    reshape x0 -> x1, local copies, waits for them, and re-layouts: none -> 5.29 us  [track_the_scales(): return jnp.concatenate(k_now, axis=on_dim)]
  transfers between devices with their start and end apart: 5 -> 5, of which waited for: 4 -> 3; matrix products, arithmetic and copies ran while one was open for 23% -> 26% of each run, Pallas kernels for 0% -> 0%
where the time goes in v1:
time: 364 us; the launch traced here: 362 us
  waiting for transfers between devices  108 us (30%)
  blocking collectives  92.5 us (25%)
  local copies, waits for them, and re-layouts  80.9 us (22%)
  matrix products  37.4 us (10%)
  other arithmetic  16 us (4%)
  between operations  14.7 us (4%)
  starting transfers between devices  12.1 us (3%)
    unnamed x1, blocking collectives  92.5 us
    all_gather x1, waiting for transfers between devices, shards(): everything = lax.all_gather(served, ('dp', 'mp'), axis=0, tiled=True)  59.9 us
    unnamed x33, local copies, waits for them, and re-layouts  45.8 us
    all_gather x1, waiting for transfers between devices, shards(): lax.all_gather(query_weight, ('dp', 'mp'), axis=0, tiled=True)  42.3 us
    all_to_all x1, starting transfers between devices, track_the_scales(): lax.all_to_all(base_arr, axis_name=a_name, split_axis=0, concat_axis=0)  11.9 us
    dot_general x1, matrix products, shards(): jnp.dot(columns, lax.all_gather(output_weight, ('dp', 'mp'), axis=0, tile...  8.85 us
    dot_general x1, matrix products, shards(): jnp.dot(columns, lax.all_gather(query_weight, ('dp', 'mp'), axis=0, tiled...  8.51 us
    dot_general x10, matrix products, one_head(): jnp.dot(weights, value_rows, preferred_element_type=jnp.float32)  8.01 us
  transfers between devices with their start and end apart: 5, of which 3 were waited for; matrix products, arithmetic and copies ran while one was open for 26% of the time, Pallas kernels for 0%

profile of v1, /device:TPU:1, one launch (start us, length us, event | category | flops | bytes accessed | tf_op | source)
XLA Modules:
  0.0 361.5 jit_solution(14453306683946297199)
XLA Ops:
  9.4 2.7 stack.2
  12.1 11.9 %all-to-all-start = ((bf16[128,20,512]{2,1,0:T(8,128)(2,1)}), bf16[128,20,512]{2,1,0:T(8,128)(2,1)}, u32[]{:S(2)}, u32[]{:S(2)}) async-start(bf16[128,20,512]{2,1,0:T(8,128)(2,1)} %stack.2), calls=%async_computation | async-start | bytes 6291456 | tf_op jit(solution)/shard_map/all_to_all | solution.py:11
  24.9 92.5 %all-reduce = s32[256]{0:T(256)S(1)} all-reduce(s32[256]{0:T(256)S(1)} %dynamic-update-slice), channel_id=1, replica_groups=mesh['dp'=8,'mp'=16] {'dp','mp'}, use_global_device_ids=true, to_apply=%add | all-reduce | flops 256 | bytes 2048
  118.3 2.7 fusion.54
  121.0 3.2 reshape.233
  125.9 5.3 %reshape.227 = bf16[2560,512]{1,0:T(8,128)(2,1)} reshape(bf16[128,20,512]{2,1,0:T(8,128)(2,1)} %all-to-all-done) | data formatting | bytes 5242880 | tf_op jit(solution)/shard_map/reshape | solution.py:12
  131.2 2.7 fusion.55
  133.9 1.3 subtract_convert_fusion.1
  135.5 1.2 pad_maximum_fusion.2
  136.6 42.3 %all-gather.11.cloned.1.call-done = bf16[128,20,2560]{2,1,0:T(8,128)(2,1)} async-done(((bf16[1,20,2560]{2,1,0:T(8,128)(2,1)}), bf16[128,20,2560]{2,1,0:T(8,128)(2,1)}) %all-gather.11.cloned.1.call-update) | async-done | bytes 13107216 | tf_op jit(solution)/shard_map/all_gather | solution.py:140
  178.9 18.0 %reshape.235 = bf16[2560,2560]{1,0:T(8,128)(2,1)} reshape(bf16[128,20,2560]{2,1,0:T(8,128)(2,1)} %all-gather.11.cloned.1.call-done) | data formatting | bytes 26214400
  196.9 8.5 %fusion.52 = f32[258,2560]{1,0:T(8,128)} fusion(bf16[2560,2560]{1,0:T(8,128)(2,1)} %reshape.235, f32[2560]{0:T(1024)S(1)} %copy-done.12, f32[258]{0:T(512)S(1)} %add_rsqrt_fusion, bf16[2,2560]{1,0:T(2,128)(2,1)S(1)} %convolution_convert_fusion.1, bf16[256,2560]{1,0:T(8,128)(2,1)S(1)} %bitcast.47), kind=kOutput, calls=%fused_computation.102 | convolution fusion | flops 3386280960 | bytes 17081352 | tf_op jit(solution)/shard_map/dot_general | solution.py:138
  205.4 4.5 %reshape.226 = f32[258,10,256]{2,1,0:T(8,128)} reshape(f32[258,2560]{1,0:T(8,128)} %fusion.52) | data formatting | bytes 5283840 | tf_op jit(solution)/shard_map/reshape | solution.py:144
  209.9 1.8 slice.140
  211.7 3.1 subtract_convert_fusion
  216.5 1.6 copy-done.6
  219.6 1.2 copy.27
  220.8 35.6 %while.10 = (s32[]{:T(128)}, bf16[10,256,256]{1,2,0:T(8,128)(2,1)}, bf16[10,256,256]{2,1,0:T(8,128)(2,1)S(1)}, bf16[2304,256]{1,0:T(8,128)(2,1)S(1)}, pred[256,2...) while((s32[]{:T(128)}, bf16[10,256,256]{1,2,0:T(8,128)(2,1)}, ...), condition=%wide.region_5.6_spmd, body=%wide.region_2.5_spmd.sunk | while | flops 609943040 | bytes 16717421 | solution.py:66
  256.4 3.5 all-gather.13.cloned.1.call-done
  259.9 18.0 %reshape.237 = bf16[2560,2560]{1,0:T(8,128)(2,1)} reshape(bf16[128,20,2560]{2,1,0:T(8,128)(2,1)} %all-gather.13.cloned.1.call-done) | data formatting | bytes 26214400
  277.9 8.8 %fusion.8 = bf16[258,2560]{1,0:T(8,128)(2,1)S(1)} fusion(bf16[2560,2560]{1,0:T(8,128)(2,1)} %reshape.237, bf16[2,2560]{0,1:T(8,128)(2,1)S(1)} %bitcast.49, bf16[256,2560]{0,1:T(8,128)(2,1)} %bitcast.55, bf16[2,2560]{1,0:T(2,128)(2,1)S(1)} %convolution_convert_fusion.1, bf16[256,2560]{1,0:T(8,128)(2,1)S(1)} %bitcast.48), kind=kOutput, calls=%fused_computation.16 | convolution fusion | flops 3388262400 | bytes 17070080 | tf_op jit(solution)/shard_map/dot_general | solution.py:153
  289.9 1.1 slice_bitcast_fusion
  291.0 59.9 %all-gather.15.cloned.1.call-done = bf16[128,2,2560]{2,1,0:T(2,128)(2,1)} async-done(((bf16[1,2,2560]{2,1,0:T(2,128)(2,1)}), bf16[128,2,2560]{2,1,0:T(2,128)(2,1)}) %all-gather.15.cloned.1.call-update) | async-done | bytes 1310736 | tf_op jit(solution)/shard_map/all_gather | solution.py:163
  350.9 3.2 reshape.239
  (145 shorter events, 47.8 us)
Async XLA Ops:
  7.2 113.8 %all-gather.9.cloned.1.call-start = ((), (), s32[]{:S(2)}) async-start(), calls=%async_computation.1 | async-start | bytes 1320960 | tf_op jit(solution)/shard_map/all_gather | solution.py:123
  7.9 171.0 %all-gather.11.cloned.1.call-start = ((), (), s32[]{:S(2)}) async-start(), calls=%async_computation.2 | async-start | bytes 15851520 | tf_op jit(solution)/shard_map/all_gather | solution.py:140
  8.6 251.3 %all-gather.13.cloned.1.call-start = ((), (), s32[]{:S(2)}) async-start(), calls=%async_computation.3 | async-start | bytes 15851520 | tf_op jit(solution)/shard_map/all_gather | solution.py:155
  12.1 12.6 %copy-start.13 = (s32[2]{0:T(128)S(1)}, s32[2]{0:T(128)}, u32[]{:S(2)}) copy-start(s32[2]{0:T(128)} %param.22) | copy-start | bytes 28
  12.1 105.4 %copy-start.11 = (s32[256]{0:T(256)S(1)}, s32[256]{0:T(256)}, u32[]{:S(2)}) copy-start(s32[256]{0:T(256)} %param.23) | copy-start | bytes 3076
  12.1 113.8 %all-to-all-start = ((bf16[128,20,512]{2,1,0:T(8,128)(2,1)}), bf16[128,20,512]{2,1,0:T(8,128)(2,1)}, u32[]{:S(2)}, u32[]{:S(2)}) async-start(bf16[128,20,512]{2,1,0:T(8,128)(2,1)} %stack.2), calls=%async_computation | async-start | bytes 6291456 | tf_op jit(solution)/shard_map/all_to_all | solution.py:11
  24.0 326.9 %all-gather.15.cloned.1.call-start = ((), (), s32[]{:S(2)}) async-start(), calls=%async_computation.4 | async-start | bytes 1320960 | tf_op jit(solution)/shard_map/all_gather | solution.py:163
  124.2 1.3 copy-start.1
  125.9 5.3 %copy-start.2 = (bf16[1,256,2560]{2,1,0:T(8,128)(2,1)S(1)}, bf16[1,256,2560]{2,1,0:T(8,128)(2,1)}, u32[]{:S(2)}) copy-start(bf16[1,256,2560]{2,1,0:T(8,128)(2,1)} %param.13) | copy-start | bytes 3932164
  125.9 5.3 %copy-start.12 = (f32[2560]{0:T(1024)S(1)}, f32[2560]{0:T(1024)}, u32[]{:S(2)}) copy-start(f32[2560]{0:T(1024)} %param.15) | copy-start | bytes 30724
  133.9 1.6 copy-start.8
  133.9 1.6 copy-start
  136.6 60.3 %copy-start.3 = (bf16[1,256,2560]{2,1,0:T(8,128)(2,1)S(1)}, bf16[1,256,2560]{2,1,0:T(8,128)(2,1)}, u32[]{:S(2)}) copy-start(bf16[1,256,2560]{2,1,0:T(8,128)(2,1)} %param.13) | copy-start | bytes 3932164
  209.9 1.8 copy-start.9
  209.9 1.8 copy-start.10
  215.9 2.3 copy-start.6
  221.5 1.3 copy-start.5
  228.6 1.3 copy-start.5
  232.1 1.4 copy-start.5
  235.8 1.3 copy-start.5
  239.4 1.3 copy-start.5
  246.5 1.3 copy-start.5
  256.4 21.5 %copy-start.4 = (bf16[1,256,2560]{2,1,0:T(8,128)(2,1)S(1)}, bf16[1,256,2560]{2,1,0:T(8,128)(2,1)}, u32[]{:S(2)}) copy-start(bf16[1,256,2560]{2,1,0:T(8,128)(2,1)} %param.13) | copy-start | bytes 3932164
  256.4 21.5 %copy-start.7 = (bf16[2,10,256]{0,2,1:T(8,128)(2,1)S(1)}, bf16[2,10,256]{0,2,1:T(8,128)(2,1)}, u32[]{:S(2)}) copy-start(bf16[2,10,256]{0,2,1:T(8,128)(2,1)} %copy.27) | copy-start | bytes 30724
  (4 other events, 5.1 us)
Sparse Core Ops, SparseCore 0:
  10.8 88.9 all-gather.8
  102.8 76.0 all-gather.10
  182.0 77.8 all-gather.12
  287.5 63.3 all-gather.14
